TPU v7x, 256 devices: a whole 4x4x8 slice. The times are simulated.
256 devices in a mesh: rows: 16 (over y, x_hi, core), feat: 16 (over z, x_lo).
Axes of the slice: x: 4 (x_hi: 2, x_lo: 2; x = x_hi * 2 + x_lo), y: 4, z: 8, core: 2. Of those that a mesh axis runs over, the one named last changes fastest.
Arguments:
- inputs: bfloat16 [32768, 512], P('rows'), may hold values from -6 to 6
- weight: bfloat16 [512, 32768], P(None, 'feat'), may hold values from -1.25 to 1.25
- phases: float32 [32768], P('feat'), may hold values from -3.140625 to 3.140625
- labels: int32 [32768], P('rows'), may hold values from 0 to 2047
- prediction: bfloat16 [32768, 2048], P('rows', 'feat'), may hold values from -4 to 4
- ridge_inverse: float32 [32768, 2048], P(('feat', 'rows')), may hold values from -2 to 2, as said below
- coefficients: float32 [32768, 2048], P(('feat', 'rows')), may hold values from -6 to 6
Outputs:
- coefficients_out: float32 [32768, 2048], P(('feat', 'rows'))
- residual_out: float32 [32768, 2048], P('rows', 'feat')
Inputs may be any that keep to these rules, and one draw needn't show every extreme that they name: `ridge_inverse`: each M_b is symmetric and positive definite.
All inputs are finite; a program needn't handle non-finite values.
Results may differ from a plain program's by a relative error of at most 0.003.
Values may be sent and summed in bfloat16 or wider, within the bound.
A program may use at most 64 MiB of HBM per device.

v0:
```python
import functools
import math

import jax
import jax.numpy as jnp
from jax import lax
from jax.experimental import pallas as pl
from jax.experimental.pallas import tpu as pltpu
from jax.sharding import PartitionSpec as P

TICKS = 4
RIDGE = 0.5
HALVES = 2

COS_POLY = (
    0.9999999890590228,
    -19.739204499453827,
    64.9391174598908,
    -85.45013953079768,
    60.16763095026347,
    -25.967599245923736,
    6.52865815775625,
)
INV_TURN = 1.0 / (2.0 * math.pi)

RS, AG1, AG2, HOP = range(4)


def nt(a, b):
    return lax.dot_general(a, b, (((1,), (1,)), ((), ())), preferred_element_type=jnp.float32)


def kernel(
    n_rows, n_feat, scale,
    x_ref, w_ref, ph_ref, lab_ref, pred_ref, m_ref, c_ref,
    cout_ref, rout_ref,
    feat, preds, dsum, rt, rs_out, rs_in, ag1, ag2, change, mcat, ct,
    send, recv, psend, precv,
):
    me = lax.axis_index("rows")
    fi = lax.axis_index("feat")
    width = pred_ref.shape[1]
    rows = x_ref.shape[0]
    fb = w_ref.shape[1]
    strip = m_ref.shape[0]
    hw = width // HALVES
    nxt = lax.rem(fi + 1, n_feat)

    barrier = pltpu.get_barrier_semaphore()

    def greet(k, _):
        pl.semaphore_signal(barrier, inc=1, device_id=(lax.rem(me + k, n_rows), fi))
        return 0

    lax.fori_loop(1, n_rows, greet, 0)
    for k in range(1, TICKS + 1):
        pl.semaphore_signal(barrier, inc=1, device_id=(me, lax.rem(fi + k, n_feat)))
        pl.semaphore_signal(barrier, inc=1, device_id=(me, lax.rem(fi + n_feat - k, n_feat)))
    pl.semaphore_wait(barrier, n_rows - 1 + 2 * TICKS)

    def turn(i, _):
        at = pl.ds(pl.multiple_of(i * 256, 256), 256)
        preds[0, :, at] = pred_ref[at, :].astype(jnp.float32).T.astype(jnp.bfloat16)
        return 0

    lax.fori_loop(0, rows // 256, turn, 0)

    def pred_copy(k):
        return pltpu.make_async_remote_copy(
            src_ref=preds.at[0],
            dst_ref=preds.at[k],
            send_sem=psend.at[k],
            recv_sem=precv.at[k],
            device_id=(me, lax.rem(fi + k, n_feat)),
        )

    for k in range(1, TICKS + 1):
        pred_copy(k).start()

    tr, tc = 256, 512

    def featurise(i, _):
        r0 = pl.ds(pl.multiple_of((i // (fb // tc)) * tr, tr), tr)
        c0 = pl.ds(pl.multiple_of(lax.rem(i, fb // tc) * tc, tc), tc)
        linear = jnp.dot(x_ref[r0, :], w_ref[:, c0], preferred_element_type=jnp.float32)
        turns = (linear + ph_ref[:, c0]) * INV_TURN
        part = turns - jnp.floor(turns + 0.5)
        u = part * part
        acc = u * (COS_POLY[-1] * scale) + COS_POLY[-2] * scale
        for a in COS_POLY[-3::-1]:
            acc = acc * u + a * scale
        feat[r0, c0] = acc.astype(jnp.bfloat16)
        return 0

    lax.fori_loop(0, (rows // tr) * (fb // tc), featurise, 0)

    high = m_ref[...].astype(jnp.bfloat16)
    mcat[0:strip, :] = high
    mcat[strip : 2 * strip, :] = (m_ref[...] - high.astype(jnp.float32)).astype(jnp.bfloat16)

    cout_ref[...] = c_ref[...]
    dsum[0] = jnp.zeros_like(dsum[0])

    def panel_columns(t):
        q = lax.rem(fi - t + n_feat, n_feat)
        return pl.ds(pl.multiple_of(q * width, width), width)

    def residual(t, h, j):
        q = lax.rem(fi - t + n_feat, n_feat)
        at = pl.ds(pl.multiple_of(j * 256, 256), 256)
        cls = lax.broadcasted_iota(jnp.int32, (hw, 256), 0) + (h * hw + q * width)
        hot = (lab_ref[:, at] == cls).astype(jnp.float32)
        return hot - preds[t, h * hw : (h + 1) * hw, at].astype(jnp.float32) - dsum[t, h, j].astype(jnp.float32)

    def gathered(buf, kind, t, h):
        return pltpu.make_async_remote_copy(
            src_ref=buf.at[t, h, pl.ds(0, n_rows - 1)],
            dst_ref=buf.at[t, h, pl.ds(0, n_rows - 1)],
            send_sem=send.at[kind, t, h],
            recv_sem=recv.at[kind, t, h],
            device_id=(lax.rem(me + 1, n_rows), fi),
        )

    def spread(buf, kind, t, h):
        def one(k, _):
            pltpu.make_async_remote_copy(
                src_ref=buf.at[t, h, me],
                dst_ref=buf.at[t, h, me],
                send_sem=send.at[kind, t, h],
                recv_sem=recv.at[kind, t, h],
                device_id=(lax.rem(me + k, n_rows), fi),
            ).start()
            return 0

        lax.fori_loop(1, n_rows, one, 0)

    def hop(t, h):
        return pltpu.make_async_remote_copy(
            src_ref=change.at[t, h],
            dst_ref=dsum.at[t + 1, h],
            send_sem=send.at[HOP, t, h],
            recv_sem=recv.at[HOP, t, h],
            device_id=(me, nxt),
        )

    def tick(t, _):
        ct[...] = c_ref[:, panel_columns(t)].T

        @pl.when(t > 0)
        def _():
            pred_copy(t).wait_recv()

        for h in range(HALVES):

            @pl.when(t > 0)
            def _():
                hop(t - 1, h).wait_recv()

            def fill(j, _):
                at = pl.ds(pl.multiple_of(j * 256, 256), 256)
                rt[h, :, at] = residual(t, h, j).astype(jnp.bfloat16)
                return 0

            lax.fori_loop(0, rows // 256, fill, 0)

            def correlate(k, _):
                pair = lax.rem(me // 2 + k, n_rows // 2)
                at = pl.ds(pl.multiple_of(pair * 2 * strip, 2 * strip), 2 * strip)
                part = jnp.dot(rt[h], feat[:, at], preferred_element_type=jnp.float32).astype(jnp.bfloat16)
                for j in range(2):
                    d = 2 * pair + j
                    rs_out[t, h, d] = part[:, j * strip : (j + 1) * strip]

                    @pl.when(d != me)
                    def _():
                        pltpu.make_async_remote_copy(
                            src_ref=rs_out.at[t, h, d],
                            dst_ref=rs_in.at[t, h, me],
                            send_sem=send.at[RS, t, h],
                            recv_sem=recv.at[RS, t, h],
                            device_id=(d, fi),
                        ).start()

                return 0

            lax.fori_loop(1, n_rows // 2 + 1, correlate, 0)
            rs_in[t, h, me] = rs_out[t, h, me]

        for h in range(HALVES):
            gathered(rs_in, RS, t, h).wait_recv()
            lanes = slice(h * hw, (h + 1) * hw)
            total = -RIDGE * ct[lanes, :]
            for s in range(n_rows):
                total = total + rs_in[t, h, s].astype(jnp.float32)
            ag1[t, h, me] = total.astype(jnp.bfloat16)
            spread(ag1, AG1, t, h)

        for h in range(HALVES):
            gathered(ag1, AG1, t, h).wait_recv()
            lanes = slice(h * hw, (h + 1) * hw)
            right = jnp.concatenate([ag1[t, h, s] for s in range(n_rows)], axis=1)
            both = nt(right, mcat[...])
            own = both[:, :strip] + both[:, strip:]
            ag2[t, h, me] = own.astype(jnp.bfloat16)
            spread(ag2, AG2, t, h)
            ct[lanes, :] = ct[lanes, :] + own

        cout_ref[:, panel_columns(t)] = ct[...].T

        for h in range(HALVES):
            gathered(ag2, AG2, t, h).wait_recv()
            delta = jnp.concatenate([ag2[t, h, s] for s in range(n_rows)], axis=1)

            def update(j, _):
                at = pl.ds(pl.multiple_of(j * 256, 256), 256)
                moved = nt(delta, feat[at, :])
                change[t, h, j] = (dsum[t, h, j].astype(jnp.float32) + moved).astype(jnp.bfloat16)
                pltpu.make_async_remote_copy(
                    src_ref=change.at[t, h, j],
                    dst_ref=dsum.at[t + 1, h, j],
                    send_sem=send.at[HOP, t, h],
                    recv_sem=recv.at[HOP, t, h],
                    device_id=(me, nxt),
                ).start()
                return 0

            lax.fori_loop(0, rows // 256, update, 0)
        return 0

    lax.fori_loop(0, TICKS, tick, 0)

    pred_copy(TICKS).wait_recv()
    for h in range(HALVES):
        hop(TICKS - 1, h).wait_recv()

    def finish(j, _):
        at = pl.ds(pl.multiple_of(j * 256, 256), 256)
        parts = [residual(TICKS, h, j) for h in range(HALVES)]
        rout_ref[at, :] = jnp.concatenate(parts, axis=0).T
        return 0

    lax.fori_loop(0, rows // 256, finish, 0)

    for k in range(1, TICKS + 1):
        pred_copy(k).wait_send()

    def drain(t, _):
        for h in range(HALVES):
            gathered(rs_out, RS, t, h).wait_send()
            gathered(ag1, AG1, t, h).wait_send()
            gathered(ag2, AG2, t, h).wait_send()
            hop(t, h).wait_send()
        return 0

    lax.fori_loop(0, TICKS, drain, 0)


def on_device(inputs, weight, phases, labels, prediction, ridge_inverse, coefficients):
    n_rows = lax.axis_size("rows")
    n_feat = lax.axis_size("feat")
    rows = inputs.shape[0]
    fb = weight.shape[1]
    width = prediction.shape[1]
    strip = ridge_inverse.shape[0]
    hw = width // HALVES
    scale = 1.0 / math.sqrt(rows * n_rows)
    bf = jnp.bfloat16
    vmem = pl.BlockSpec(memory_space=pltpu.VMEM)
    pieces = (TICKS, HALVES, n_rows, hw, strip)
    return pl.pallas_call(
        functools.partial(kernel, n_rows, n_feat, scale),
        out_shape=(
            jax.ShapeDtypeStruct(coefficients.shape, jnp.float32),
            jax.ShapeDtypeStruct(prediction.shape, jnp.float32),
        ),
        in_specs=[vmem] * 7,
        out_specs=(vmem, vmem),
        scratch_shapes=[
            pltpu.VMEM((rows, fb), bf),
            pltpu.VMEM((TICKS + 1, width, rows), bf),
            pltpu.VMEM((TICKS + 1, HALVES, rows // 256, hw, 256), bf),
            pltpu.VMEM((HALVES, hw, rows), bf),
            pltpu.VMEM(pieces, bf),
            pltpu.VMEM(pieces, bf),
            pltpu.VMEM(pieces, bf),
            pltpu.VMEM(pieces, bf),
            pltpu.VMEM((TICKS, HALVES, rows // 256, hw, 256), bf),
            pltpu.VMEM((2 * strip, fb), bf),
            pltpu.VMEM((width, strip), jnp.float32),
            pltpu.SemaphoreType.DMA((4, TICKS, HALVES)),
            pltpu.SemaphoreType.DMA((4, TICKS, HALVES)),
            pltpu.SemaphoreType.DMA((TICKS + 1,)),
            pltpu.SemaphoreType.DMA((TICKS + 1,)),
        ],
        compiler_params=pltpu.CompilerParams(
            collective_id=0, has_side_effects=True, vmem_limit_bytes=60 * 2**20
        ),
    )(
        inputs,
        weight,
        phases.reshape(1, -1),
        labels.reshape(1, -1),
        prediction,
        ridge_inverse,
        coefficients,
    )


def solution(mesh):
    placed = (
        P("rows", None),
        P(None, "feat"),
        P("feat"),
        P("rows"),
        P("rows", "feat"),
        P(("feat", "rows"), None),
        P(("feat", "rows"), None),
    )
    return jax.shard_map(
        on_device,
        mesh=mesh,
        in_specs=placed,
        out_specs=(P(("feat", "rows"), None), P("rows", "feat")),
        check_vma=False,
    )
```

profile of v0, /device:TPU:161, one launch (start us, length us, event | category | flops | bytes accessed | tf_op | source)
XLA Modules:
  0.0 205.5 jit_solution(12003129814434823728)
XLA Ops:
  0.6 201.5 %shard_map.86 = (f32[128,2048]{1,0:T(8,128)}, f32[2048,128]{1,0:T(8,128)}) custom-call(bf16[2048,512]{1,0:T(8,128)(2,1)} %x_ref.1, bf16[512,2048]{1,0:T(8,128)(2,1)} %w_ref.1, f32[1,2048]{1,0:T(1,128)} %bitcast.2, s32[1,2048]{1,0:T(1,128)} %bitcast.3, bf16[2048,128]{1,0:T(8,128)(2,1)} %pred_ref.1, f32[128,2048]{1,0:T(8,128)} %m_ref.1, f32[128,2048]{1,0:T(8,128)} %c_ref.1), custom_call_target="tpu_custom_call" | custom-call | tf_op jit(solution)/shard_map/pallas_call | solution.py:270
  202.1 0.0 copy-start
  202.1 2.4 %copy.11 = f32[128,2048]{1,0:T(8,128)} copy(f32[128,2048]{1,0:T(8,128)} %get-tuple-element.4) | data formatting | bytes 2097152
  204.5 0.0 copy-done
  204.5 1.0 copy.12
Async XLA Ops:
  202.1 2.4 %copy-start = (f32[2048,128]{1,0:T(8,128)S(1)}, f32[2048,128]{1,0:T(8,128)}, u32[]{:S(2)}) copy-start(f32[2048,128]{1,0:T(8,128)} %get-tuple-element.5) | copy-start | bytes 3145732
where the time goes:
time: 206 us; the launch traced here: 205 us
  Pallas kernels  201 us (98%)
  local copies, waits for them, and re-layouts  3.36 us (2%)
    pallas_call x1, Pallas kernels, on_device(): pl.pallas_call(functools.partial(kernel, n_rows, n_feat, scale), out_shap...  201 us

commit v1 on v0

v1 whole, which is shorter than its diff:
```python
import functools
import math

import jax
import jax.numpy as jnp
from jax import lax
from jax.experimental import pallas as pl
from jax.experimental.pallas import tpu as pltpu
from jax.sharding import PartitionSpec as P

TICKS = 4
RIDGE = 0.5
HALVES = 2
CHUNKS = 8

COS_POLY = (
    0.9999999890590228,
    -19.739204499453827,
    64.9391174598908,
    -85.45013953079768,
    60.16763095026347,
    -25.967599245923736,
    6.52865815775625,
)
INV_TURN = 1.0 / (2.0 * math.pi)

RS, RIGHT, AG = range(3)


def nt(a, b):
    return lax.dot_general(a, b, (((1,), (1,)), ((), ())), preferred_element_type=jnp.float32)


def kernel(
    n_rows, n_feat, n_y, scale,
    x_ref, w_ref, ph_ref, lab_ref, pred_ref, m_ref, c_ref,
    cout_ref, rout_ref,
    feat, preds, dsum, acc, rs_out, rs_in, right, ag, change, mcat, ctn,
    send, recv, hsend, hrecv, psend, precv, msend, mrecv,
):
    me = lax.axis_index("rows")
    fi = lax.axis_index("feat")
    n_b = n_rows // n_y
    my_y = me // n_b
    my_b = lax.rem(me, n_b)
    sibling = me + 1 - 2 * lax.rem(me, 2)
    core = lax.rem(me, 2)
    chip = me // 2
    n_chip = n_rows // 2
    width = pred_ref.shape[1]
    rows = x_ref.shape[0]
    fb = w_ref.shape[1]
    strip = m_ref.shape[0]
    hw = width // HALVES
    cw = hw // 2
    block = fb // n_chip
    chunk = rows // CHUNKS
    nxt = lax.rem(fi + 1, n_feat)

    offsets = [(dy, db) for dy in (2, 1, 3, 0) for db in (2, 3, 1, 0)]

    def place(dy, db):
        return lax.rem(my_y + dy, n_y) * n_b + lax.rem(my_b + db, n_b)

    barrier = pltpu.get_barrier_semaphore()
    for dy, db in offsets[:-1]:
        pl.semaphore_signal(barrier, inc=1, device_id=(place(dy, db), fi))
    for k in (1, 2):
        pl.semaphore_signal(barrier, inc=1, device_id=(me, lax.rem(fi + k, n_feat)))
        pl.semaphore_signal(barrier, inc=1, device_id=(me, lax.rem(fi + n_feat - k, n_feat)))
    pl.semaphore_wait(barrier, n_rows - 1 + 4)

    own_rows = pl.ds(pl.multiple_of(core * strip, strip), strip)
    high = m_ref[...].astype(jnp.bfloat16)
    mcat[0, own_rows, :] = high
    mcat[1, own_rows, :] = (m_ref[...] - high.astype(jnp.float32)).astype(jnp.bfloat16)
    ridge_copy = pltpu.make_async_remote_copy(
        src_ref=mcat.at[:, own_rows],
        dst_ref=mcat.at[:, own_rows],
        send_sem=msend,
        recv_sem=mrecv,
        device_id=(sibling, fi),
    )
    ridge_copy.start()

    def turn(i, _):
        at = pl.ds(pl.multiple_of(i * 256, 256), 256)
        preds[0, :, at] = pred_ref[at, :].astype(jnp.float32).T.astype(jnp.bfloat16)
        return 0

    lax.fori_loop(0, rows // 256, turn, 0)

    def pred_copy(k):
        return pltpu.make_async_remote_copy(
            src_ref=preds.at[max(k - 2, 0)],
            dst_ref=preds.at[k],
            send_sem=psend.at[k],
            recv_sem=precv.at[k],
            device_id=(me, lax.rem(fi + min(k, 2), n_feat)),
        )

    pred_copy(1).start()
    pred_copy(2).start()

    tc = 256

    def featurise(i, _):
        c0 = pl.ds(pl.multiple_of(i * tc, tc), tc)
        linear = jnp.dot(x_ref[...], w_ref[:, c0], preferred_element_type=jnp.float32)
        turns = linear * INV_TURN + ph_ref[:, c0] * INV_TURN
        part = turns - jnp.round(turns)
        u = part * part
        value = u * (COS_POLY[-1] * scale) + COS_POLY[-2] * scale
        for a in COS_POLY[-3::-1]:
            value = value * u + a * scale
        feat[:, c0] = value.astype(jnp.bfloat16)
        return 0

    lax.fori_loop(0, fb // tc, featurise, 0)

    dsum[0] = jnp.zeros_like(dsum[0])

    def panel(t):
        return lax.rem(fi - t + n_feat, n_feat)

    def panel_columns(t):
        return pl.ds(pl.multiple_of(panel(t) * width, width), width)

    def residual(t, h, j):
        at = pl.ds(pl.multiple_of(j * chunk, chunk), chunk)
        cls = lax.broadcasted_iota(jnp.int32, (hw, chunk), 0) + (h * hw + panel(t) * width)
        hot = (lab_ref[:, at] == cls).astype(jnp.float32)
        return hot - preds[t, h * hw : (h + 1) * hw, at].astype(jnp.float32) - dsum[t, h, j].astype(jnp.float32)

    def to_place(kind, t, h, src, dst, device):
        return pltpu.make_async_remote_copy(
            src_ref=src,
            dst_ref=dst,
            send_sem=send.at[kind, t, h],
            recv_sem=recv.at[kind, t, h],
            device_id=(device, fi),
        )

    def all_of(kind, t, h, buf, count):
        some = buf.at[t, h, pl.ds(0, count)]
        return to_place(kind, t, h, some, some, sibling)

    def hop(t, h, j):
        return pltpu.make_async_remote_copy(
            src_ref=change.at[t, h, j],
            dst_ref=dsum.at[t + 1, h, j],
            send_sem=hsend.at[t, h, j],
            recv_sem=hrecv.at[t, h, j],
            device_id=(me, nxt),
        )

    def correlate(t, h):
        acc[...] = jnp.zeros_like(acc)
        cols = panel_columns(t)
        mine = pl.ds(pl.multiple_of(me * strip, strip), strip)
        acc[:, mine] = -RIDGE * c_ref[:, cols].T[h * hw : (h + 1) * hw, :]

        def arrived(j):
            @pl.when(t > 0)
            def _():
                hop(t - 1, h, j).wait_recv()

            return residual(t, h, j).astype(jnp.bfloat16)

        def first(j, _):
            part = arrived(j)
            r0 = pl.ds(pl.multiple_of(j * chunk, chunk), chunk)
            acc[...] = acc[...] + jnp.dot(part, feat[r0, :], preferred_element_type=jnp.float32)
            return 0

        lax.fori_loop(0, CHUNKS - 1, first, 0)
        last = arrived(CHUNKS - 1)
        for dy in (2, 1, 3, 0):
            y = lax.rem(my_y + dy, n_y)
            c0 = pl.ds(pl.multiple_of(y * 2 * block, 2 * block), 2 * block)
            total = acc[:, c0] + jnp.dot(
                last, feat[rows - chunk : rows, c0], preferred_element_type=jnp.float32
            )
            total = total.astype(jnp.bfloat16)
            for b in range(n_b):
                lanes = slice(b // 2 * block, (b // 2 + 1) * block)
                rs_out[t, h, y * n_b + b] = total[b % 2 * cw : (b % 2 + 1) * cw, lanes]
            for db in (2, 3, 1, 0):
                if (dy, db) != (0, 0):
                    d = place(dy, db)
                    to_place(RS, t, h, rs_out.at[t, h, d], rs_in.at[t, h, me], d).start()
        rs_in[t, h, me] = rs_out[t, h, me]

    def collect(t, h):
        all_of(RS, t, h, rs_in, n_rows - 1).wait_recv()
        total = rs_in[t, h, 0].astype(jnp.float32)
        for s in range(1, n_rows):
            total = total + rs_in[t, h, s].astype(jnp.float32)
        right[t, h, chip] = total.astype(jnp.bfloat16)
        for dy, db in offsets[:-1]:
            if db % 2 == 0:
                mine = right.at[t, h, chip]
                to_place(RIGHT, t, h, mine, mine, place(dy, db)).start()

    def solve(t, h):
        all_of(RIGHT, t, h, right, n_chip - 1).wait_recv()
        whole = jnp.concatenate([right[t, h, a] for a in range(n_chip)], axis=1)
        own = nt(whole, mcat[0]) + nt(whole, mcat[1])
        ag[t, h, me] = own.astype(jnp.bfloat16)
        for dy, db in offsets[:-1]:
            to_place(AG, t, h, ag.at[t, h, me], ag.at[t, h, me], place(dy, db)).start()

    def update(t, h):
        all_of(AG, t, h, ag, n_rows - 1).wait_recv()
        delta = jnp.concatenate(
            [
                jnp.concatenate([ag[t, h, 2 * a + c] for a in range(n_chip)], axis=1)
                for c in range(2)
            ],
            axis=0,
        )

        def moved(j, _):
            at = pl.ds(pl.multiple_of(j * chunk, chunk), chunk)
            total = dsum[t, h, j].astype(jnp.float32) + nt(delta, feat[at, :])
            change[t, h, j] = total.astype(jnp.bfloat16)
            hop(t, h, j).start()
            return 0

        lax.fori_loop(0, CHUNKS, moved, 0)
        for c in range(2):
            lanes = slice(h * hw + c * cw, h * hw + (c + 1) * cw)
            ctn[t, lanes, :] = ag[t, h, 2 * chip + c, :, own_rows].astype(jnp.float32)

    correlate(0, 0)
    correlate(0, 1)
    ridge_copy.wait_recv()
    pred_copy(1).wait_recv()
    pred_copy(3).start()

    def tick(t, _):
        for h in range(HALVES):
            collect(t, h)
        for h in range(HALVES):
            solve(t, h)

        @pl.when(t == 1)
        def _():
            pred_copy(2).wait_recv()
            pred_copy(4).start()

        for h in range(HALVES):
            update(t, h)

        @pl.when(t == 2)
        def _():
            pred_copy(3).wait_recv()

        @pl.when(t < TICKS - 1)
        def _():
            for h in range(HALVES):
                correlate(t + 1, h)

        return 0

    lax.fori_loop(0, TICKS, tick, 0)

    for t in range(TICKS):
        cols = panel_columns(t)
        if t == 0:
            cout_ref[...] = c_ref[...]
        cout_ref[:, cols] = c_ref[:, cols] + ctn[t].T

    pred_copy(TICKS).wait_recv()

    for j in range(CHUNKS):
        for h in range(HALVES):
            hop(TICKS - 1, h, j).wait_recv()
        parts = [residual(TICKS, h, j) for h in range(HALVES)]
        rout_ref[j * chunk : (j + 1) * chunk, :] = jnp.concatenate(parts, axis=0).T

    for k in range(1, TICKS + 1):
        pred_copy(k).wait_send()
    ridge_copy.wait_send()

    def drain(t, _):
        for h in range(HALVES):
            all_of(RS, t, h, rs_out, n_rows - 1).wait_send()
            all_of(RIGHT, t, h, right, n_chip - 1).wait_send()
            all_of(AG, t, h, ag, n_rows - 1).wait_send()
            for j in range(CHUNKS):
                hop(t, h, j).wait_send()
        return 0

    lax.fori_loop(0, TICKS, drain, 0)


def on_device(inputs, weight, phases, labels, prediction, ridge_inverse, coefficients):
    n_rows = lax.axis_size("rows")
    n_feat = lax.axis_size("feat")
    n_y = 4
    rows = inputs.shape[0]
    fb = weight.shape[1]
    width = prediction.shape[1]
    strip = ridge_inverse.shape[0]
    hw = width // HALVES
    block = 2 * fb // n_rows
    cw = hw // 2
    scale = 1.0 / math.sqrt(rows * n_rows)
    bf = jnp.bfloat16
    vmem = pl.BlockSpec(memory_space=pltpu.VMEM)
    pieces = (TICKS, HALVES, n_rows, cw, block)
    return pl.pallas_call(
        functools.partial(kernel, n_rows, n_feat, n_y, scale),
        name="ridge",
        out_shape=(
            jax.ShapeDtypeStruct(coefficients.shape, jnp.float32),
            jax.ShapeDtypeStruct(prediction.shape, jnp.float32),
        ),
        in_specs=[vmem] * 7,
        out_specs=(vmem, vmem),
        scratch_shapes=[
            pltpu.VMEM((rows, fb), bf),
            pltpu.VMEM((TICKS + 1, width, rows), bf),
            pltpu.VMEM((TICKS + 1, HALVES, CHUNKS, hw, rows // CHUNKS), bf),
            pltpu.VMEM((hw, fb), jnp.float32),
            pltpu.VMEM(pieces, bf),
            pltpu.VMEM(pieces, bf),
            pltpu.VMEM((TICKS, HALVES, n_rows // 2, cw, block), bf),
            pltpu.VMEM(pieces, bf),
            pltpu.VMEM((TICKS, HALVES, CHUNKS, hw, rows // CHUNKS), bf),
            pltpu.VMEM((2, 2 * strip, fb), bf),
            pltpu.VMEM((TICKS, width, strip), jnp.float32),
            pltpu.SemaphoreType.DMA((3, TICKS, HALVES)),
            pltpu.SemaphoreType.DMA((3, TICKS, HALVES)),
            pltpu.SemaphoreType.DMA((TICKS, HALVES, CHUNKS)),
            pltpu.SemaphoreType.DMA((TICKS, HALVES, CHUNKS)),
            pltpu.SemaphoreType.DMA((TICKS + 1,)),
            pltpu.SemaphoreType.DMA((TICKS + 1,)),
            pltpu.SemaphoreType.DMA,
            pltpu.SemaphoreType.DMA,
        ],
        compiler_params=pltpu.CompilerParams(
            collective_id=0, has_side_effects=True, vmem_limit_bytes=60 * 2**20
        ),
    )(
        inputs,
        weight,
        phases.reshape(1, -1),
        labels.reshape(1, -1),
        prediction,
        ridge_inverse,
        coefficients,
    )


def solution(mesh):
    placed = (
        P("rows", None),
        P(None, "feat"),
        P("feat"),
        P("rows"),
        P("rows", "feat"),
        P(("feat", "rows"), None),
        P(("feat", "rows"), None),
    )
    return jax.shard_map(
        on_device,
        mesh=mesh,
        in_specs=placed,
        out_specs=(P(("feat", "rows"), None), P("rows", "feat")),
        check_vma=False,
    )
```

time: 206 us -> 167 us (0.81)
  the two profiles are of different devices: /device:TPU:161 before, /device:TPU:1 now
where the time goes in v1:
time: 167 us; the launch traced here: 165 us
  Pallas kernels  161 us (96%)
  local copies, waits for them, and re-layouts  3.36 us (2%)
    pallas_call x1, Pallas kernels, on_device(): pl.pallas_call(functools.partial(kernel, n_rows, n_feat, n_y, scale), nam...  161 us
    unnamed x4, local copies, waits for them, and re-layouts  3.36 us

profile of v1, /device:TPU:1, one launch (start us, length us, event | category | flops | bytes accessed | tf_op | source)
XLA Modules:
  0.0 164.8 jit_solution(386262323514612962)
XLA Ops:
  0.6 160.8 %ridge.1 = (f32[128,2048]{1,0:T(8,128)}, f32[2048,128]{1,0:T(8,128)}) custom-call(bf16[2048,512]{1,0:T(8,128)(2,1)} %x_ref.1, bf16[512,2048]{1,0:T(8,128)(2,1)} %w_ref.1, f32[1,2048]{1,0:T(1,128)} %bitcast.2, s32[1,2048]{1,0:T(1,128)} %bitcast.3, bf16[2048,128]{1,0:T(8,128)(2,1)} %pred_ref.1, f32[128,2048]{1,0:T(8,128)} %m_ref.1, f32[128,2048]{1,0:T(8,128)} %c_ref.1), custom_call_target="tpu_custom_call" | custom-call | tf_op jit(solution)/shard_map/ridge/pallas_call | solution.py:313
  161.4 0.0 copy-start
  161.4 2.4 %copy.11 = f32[128,2048]{1,0:T(8,128)} copy(f32[128,2048]{1,0:T(8,128)} %get-tuple-element.4) | data formatting | bytes 2097152
  163.8 0.0 copy-done
  163.8 1.0 copy.12
Async XLA Ops:
  161.4 2.4 %copy-start = (f32[2048,128]{1,0:T(8,128)S(1)}, f32[2048,128]{1,0:T(8,128)}, u32[]{:S(2)}) copy-start(f32[2048,128]{1,0:T(8,128)} %get-tuple-element.5) | copy-start | bytes 3145732

commit v2 on v1

--- a/solution.py
+++ b/solution.py
@@ -35,8 +35,8 @@
     n_rows, n_feat, n_y, scale,
     x_ref, w_ref, ph_ref, lab_ref, pred_ref, m_ref, c_ref,
     cout_ref, rout_ref,
-    feat, preds, dsum, acc, rs_out, rs_in, right, ag, change, mcat, ctn,
-    send, recv, hsend, hrecv, psend, precv, msend, mrecv,
+    feat, preds, dsum, acc, m_own, rs_out, rs_in, right, ag, change, mcat, ctn,
+    send, recv, hsend, hrecv, psend, precv, msend, mrecv, loads,
 ):
     me = lax.axis_index("rows")
     fi = lax.axis_index("feat")
@@ -62,6 +62,11 @@
     def place(dy, db):
         return lax.rem(my_y + dy, n_y) * n_b + lax.rem(my_b + db, n_b)
 
+    m_load = pltpu.make_async_copy(m_ref, m_own, loads.at[0])
+    c_load = pltpu.make_async_copy(c_ref, cout_ref, loads.at[1])
+    m_load.start()
+    c_load.start()
+
     barrier = pltpu.get_barrier_semaphore()
     for dy, db in offsets[:-1]:
         pl.semaphore_signal(barrier, inc=1, device_id=(place(dy, db), fi))
@@ -71,18 +76,6 @@
     pl.semaphore_wait(barrier, n_rows - 1 + 4)
 
     own_rows = pl.ds(pl.multiple_of(core * strip, strip), strip)
-    high = m_ref[...].astype(jnp.bfloat16)
-    mcat[0, own_rows, :] = high
-    mcat[1, own_rows, :] = (m_ref[...] - high.astype(jnp.float32)).astype(jnp.bfloat16)
-    ridge_copy = pltpu.make_async_remote_copy(
-        src_ref=mcat.at[:, own_rows],
-        dst_ref=mcat.at[:, own_rows],
-        send_sem=msend,
-        recv_sem=mrecv,
-        device_id=(sibling, fi),
-    )
-    ridge_copy.start()
-
     def turn(i, _):
         at = pl.ds(pl.multiple_of(i * 256, 256), 256)
         preds[0, :, at] = pred_ref[at, :].astype(jnp.float32).T.astype(jnp.bfloat16)
@@ -158,7 +151,7 @@
         acc[...] = jnp.zeros_like(acc)
         cols = panel_columns(t)
         mine = pl.ds(pl.multiple_of(me * strip, strip), strip)
-        acc[:, mine] = -RIDGE * c_ref[:, cols].T[h * hw : (h + 1) * hw, :]
+        acc[:, mine] = -RIDGE * cout_ref[:, cols].T[h * hw : (h + 1) * hw, :]
 
         def arrived(j):
             @pl.when(t > 0)
@@ -232,13 +225,30 @@
             lanes = slice(h * hw + c * cw, h * hw + (c + 1) * cw)
             ctn[t, lanes, :] = ag[t, h, 2 * chip + c, :, own_rows].astype(jnp.float32)
 
+    c_load.wait()
     correlate(0, 0)
     correlate(0, 1)
+    m_load.wait()
+    high = m_own[...].astype(jnp.bfloat16)
+    mcat[0, own_rows, :] = high
+    mcat[1, own_rows, :] = (m_own[...] - high.astype(jnp.float32)).astype(jnp.bfloat16)
+    ridge_copy = pltpu.make_async_remote_copy(
+        src_ref=mcat.at[:, own_rows],
+        dst_ref=mcat.at[:, own_rows],
+        send_sem=msend,
+        recv_sem=mrecv,
+        device_id=(sibling, fi),
+    )
+    ridge_copy.start()
     ridge_copy.wait_recv()
     pred_copy(1).wait_recv()
     pred_copy(3).start()
 
     def tick(t, _):
+        @pl.when(t == 2)
+        def _():
+            pred_copy(4).start()
+
         for h in range(HALVES):
             collect(t, h)
         for h in range(HALVES):
@@ -247,7 +257,6 @@
         @pl.when(t == 1)
         def _():
             pred_copy(2).wait_recv()
-            pred_copy(4).start()
 
         for h in range(HALVES):
             update(t, h)
@@ -267,9 +276,7 @@
 
     for t in range(TICKS):
         cols = panel_columns(t)
-        if t == 0:
-            cout_ref[...] = c_ref[...]
-        cout_ref[:, cols] = c_ref[:, cols] + ctn[t].T
+        cout_ref[:, cols] = cout_ref[:, cols] + ctn[t].T
 
     pred_copy(TICKS).wait_recv()
 
@@ -317,13 +324,14 @@
             jax.ShapeDtypeStruct(coefficients.shape, jnp.float32),
             jax.ShapeDtypeStruct(prediction.shape, jnp.float32),
         ),
-        in_specs=[vmem] * 7,
+        in_specs=[vmem] * 5 + [pl.BlockSpec(memory_space=pl.ANY)] * 2,
         out_specs=(vmem, vmem),
         scratch_shapes=[
             pltpu.VMEM((rows, fb), bf),
             pltpu.VMEM((TICKS + 1, width, rows), bf),
             pltpu.VMEM((TICKS + 1, HALVES, CHUNKS, hw, rows // CHUNKS), bf),
             pltpu.VMEM((hw, fb), jnp.float32),
+            pltpu.VMEM((strip, fb), jnp.float32),
             pltpu.VMEM(pieces, bf),
             pltpu.VMEM(pieces, bf),
             pltpu.VMEM((TICKS, HALVES, n_rows // 2, cw, block), bf),
@@ -339,6 +347,7 @@
             pltpu.SemaphoreType.DMA((TICKS + 1,)),
             pltpu.SemaphoreType.DMA,
             pltpu.SemaphoreType.DMA,
+            pltpu.SemaphoreType.DMA((2,)),
         ],
         compiler_params=pltpu.CompilerParams(
             collective_id=0, has_side_effects=True, vmem_limit_bytes=60 * 2**20

time: 167 us -> 157 us (0.940)
  Pallas kernels: 161 us -> 152 us
    pallas_call x1, Pallas kernels: 161 us -> 152 us  [on_device(): pl.pallas_call(functools.partial(kernel, n_rows, n_feat, n_y, scale), nam...]
where the time goes in v2:
time: 157 us; the launch traced here: 156 us
  Pallas kernels  152 us (97%)
  local copies, waits for them, and re-layouts  3.36 us (2%)
    pallas_call x1, Pallas kernels, on_device(): pl.pallas_call(functools.partial(kernel, n_rows, n_feat, n_y, scale), nam...  152 us
    unnamed x4, local copies, waits for them, and re-layouts  3.36 us

profile of v2, /device:TPU:1, one launch (start us, length us, event | category | flops | bytes accessed | tf_op | source)
XLA Modules:
  0.0 156.5 jit_solution(7942356153793023954)
XLA Ops:
  0.6 152.5 %ridge.1 = (f32[128,2048]{1,0:T(8,128)}, f32[2048,128]{1,0:T(8,128)}) custom-call(bf16[2048,512]{1,0:T(8,128)(2,1)} %x_ref.1, bf16[512,2048]{1,0:T(8,128)(2,1)} %w_ref.1, f32[1,2048]{1,0:T(1,128)} %bitcast.2, s32[1,2048]{1,0:T(1,128)} %bitcast.3, bf16[2048,128]{1,0:T(8,128)(2,1)} %pred_ref.1, f32[128,2048]{1,0:T(8,128)} %m_ref.1, f32[128,2048]{1,0:T(8,128)} %c_ref.1), custom_call_target="tpu_custom_call" | custom-call | tf_op jit(solution)/shard_map/ridge/pallas_call | solution.py:320
  153.1 0.0 copy-start
  153.1 2.4 %copy.11 = f32[128,2048]{1,0:T(8,128)} copy(f32[128,2048]{1,0:T(8,128)} %get-tuple-element.4) | data formatting | bytes 2097152
  155.5 0.0 copy-done
  155.5 1.0 copy.12
Async XLA Ops:
  153.1 2.4 %copy-start = (f32[2048,128]{1,0:T(8,128)S(1)}, f32[2048,128]{1,0:T(8,128)}, u32[]{:S(2)}) copy-start(f32[2048,128]{1,0:T(8,128)} %get-tuple-element.5) | copy-start | bytes 3145732

commit v3 on v2

--- a/solution.py
+++ b/solution.py
@@ -73,9 +73,6 @@
     for k in (1, 2):
         pl.semaphore_signal(barrier, inc=1, device_id=(me, lax.rem(fi + k, n_feat)))
         pl.semaphore_signal(barrier, inc=1, device_id=(me, lax.rem(fi + n_feat - k, n_feat)))
-    pl.semaphore_wait(barrier, n_rows - 1 + 4)
-
-    own_rows = pl.ds(pl.multiple_of(core * strip, strip), strip)
     def turn(i, _):
         at = pl.ds(pl.multiple_of(i * 256, 256), 256)
         preds[0, :, at] = pred_ref[at, :].astype(jnp.float32).T.astype(jnp.bfloat16)
@@ -83,6 +80,9 @@
 
     lax.fori_loop(0, rows // 256, turn, 0)
 
+    pl.semaphore_wait(barrier, n_rows - 1 + 4)
+
+    own_rows = pl.ds(pl.multiple_of(core * strip, strip), strip)
     def pred_copy(k):
         return pltpu.make_async_remote_copy(
             src_ref=preds.at[max(k - 2, 0)],

time: 157 us -> 156 us (level)
  no operation moved by 1% of the time
where the time goes in v3:
time: 156 us
  Pallas kernels  152 us (97%)
  local copies, waits for them, and re-layouts  3.36 us (2%)
    pallas_call x1, Pallas kernels, on_device(): pl.pallas_call(functools.partial(kernel, n_rows, n_feat, n_y, scale), nam...  152 us
    unnamed x4, local copies, waits for them, and re-layouts  3.36 us

profile of v3, /device:TPU:1, one launch (start us, length us, event | category | flops | bytes accessed | tf_op | source)
XLA Modules:
  0.0 155.8 jit_solution(17669730933839081105)
XLA Ops:
  0.6 151.8 %ridge.1 = (f32[128,2048]{1,0:T(8,128)}, f32[2048,128]{1,0:T(8,128)}) custom-call(bf16[2048,512]{1,0:T(8,128)(2,1)} %x_ref.1, bf16[512,2048]{1,0:T(8,128)(2,1)} %w_ref.1, f32[1,2048]{1,0:T(1,128)} %bitcast.2, s32[1,2048]{1,0:T(1,128)} %bitcast.3, bf16[2048,128]{1,0:T(8,128)(2,1)} %pred_ref.1, f32[128,2048]{1,0:T(8,128)} %m_ref.1, f32[128,2048]{1,0:T(8,128)} %c_ref.1), custom_call_target="tpu_custom_call" | custom-call | tf_op jit(solution)/shard_map/ridge/pallas_call | solution.py:320
  152.4 0.0 copy-start
  152.4 2.4 %copy.11 = f32[128,2048]{1,0:T(8,128)} copy(f32[128,2048]{1,0:T(8,128)} %get-tuple-element.4) | data formatting | bytes 2097152
  154.8 0.0 copy-done
  154.8 1.0 copy.12
Async XLA Ops:
  152.4 2.4 %copy-start = (f32[2048,128]{1,0:T(8,128)S(1)}, f32[2048,128]{1,0:T(8,128)}, u32[]{:S(2)}) copy-start(f32[2048,128]{1,0:T(8,128)} %get-tuple-element.5) | copy-start | bytes 3145732
